TPU v7x, 32 devices: a whole 2x2x4 slice. The times are simulated.
32 devices in a mesh: parts: 2 (over x), tm: 16 (over z, y, core).
Axes of the slice: x: 2, y: 2, z: 4, core: 2. Of those that a mesh axis runs over, the one named last changes fastest.
Arguments:
- currents: bfloat16 [49152, 1024], P('tm', 'parts'), parts along dimension 1, may hold values from -5 to 5
- seed_on_tension: bfloat16 [49152, 1024], P('tm', 'parts'), parts along dimension 1, may hold values from -6 to 6
- mode_diffusivity_factor: float32 [32, 98304], P(None, ('parts', 'tm')), parts along dimension 1, may hold values from 0.25 to 34410
- decay_rates: float32 [32], replicated, may hold values from 6.1035156e-06 to 0.34
- fit_weights: float32 [32], replicated, may hold values from 0.06 to 0.3
- counts: int32 [1024], P('parts'), parts along dimension 0, may hold values from 1 to 16
Outputs:
- tension_at_end: bfloat16 [49152, 1024], P('tm', 'parts'), parts along dimension 1
- gradient_wrt_draw: bfloat16 [49152, 1024], P('tm', 'parts'), parts along dimension 1
- softened_peak_tension: float32 [1024], P('parts'), parts along dimension 0
There are 2 independent parts, one for each index of `parts`. A program takes and returns all parts, laid end to end along the dimension named above; an argument that names none is the same for every part. Nothing has to cross between parts.
All inputs are finite; a program needn't handle non-finite values.
Results may differ from a plain program's by a relative error of at most 0.0053.
Values sent between devices are 32-bit elements; how exact they have to be, the bound alone decides.
No kernel may reach another device: no remote copies, remote signals or barrier semaphores. Data moves between devices by JAX's collectives and lax.ppermute only.
A program may use at most 192 MiB of HBM per device.

v0:
```python
import jax
import jax.numpy as jnp
from jax import lax
from jax.sharding import PartitionSpec as P

KERNEL_SPAN = 768
SHARPNESS = 4.0
FAR_AWAY = 1e30


def entering(part, axis, combine, identity, reverse):
    count = lax.axis_size(axis)
    place = lax.axis_index(axis)
    ahead = count - 1 - place if reverse else place
    gathered = jax.tree.map(lambda a: lax.all_gather(a, axis), part)
    state = jax.tree.map(lambda a, e: jnp.zeros_like(a) + jnp.asarray(e, a.dtype), part, identity)

    def one(hop, state):
        source = count - 1 - hop if reverse else hop
        return combine(
            state, jax.tree.map(lambda a: lax.dynamic_index_in_dim(a, source, 0, False), gathered)
        )

    return lax.fori_loop(0, ahead, one, state)


def combine_states(earlier, latter):
    return (earlier[0] * latter[0], latter[0][:, None] * earlier[1] + latter[1])


def body(currents, seed_on_tension, mode_diffusivity_factor, decay_rates, fit_weights, counts):
    samples, conductor_total = currents.shape
    kernel_spans = samples // KERNEL_SPAN
    mode_count = decay_rates.shape[0]
    mode_gains = fit_weights * jnp.sqrt(decay_rates)
    length_scale = counts.astype(jnp.float32) / 4.0
    prefix = jnp.cumsum(
        mode_diffusivity_factor.reshape(mode_count, kernel_spans, KERNEL_SPAN), axis=2
    ).transpose(1, 0, 2)
    closing_instant = prefix[:, :, -1]
    prefix_rows = prefix.transpose(0, 2, 1)
    row_ids = lax.broadcasted_iota(jnp.int32, (KERNEL_SPAN, KERNEL_SPAN), 0)
    col_ids = lax.broadcasted_iota(jnp.int32, (KERNEL_SPAN, KERNEL_SPAN), 1)
    lower_part = (row_ids >= col_ids)[None]
    kernel_list = []
    for position in range(kernel_spans):
        block_kernel = jnp.zeros((KERNEL_SPAN, KERNEL_SPAN), jnp.float32)
        for first_mode in range(0, mode_count, 8):
            rate_part = decay_rates[first_mode : first_mode + 8]
            gain_part = mode_gains[first_mode : first_mode + 8]
            part_prefix = prefix[position, first_mode : first_mode + 8]
            spread = part_prefix[:, :, None] - part_prefix[:, None, :]
            spread = jnp.where(lower_part, spread, FAR_AWAY)
            block_kernel = block_kernel + jnp.sum(
                gain_part[:, None, None] * jnp.exp(-rate_part[:, None, None] * spread), axis=0
            )
        kernel_list.append(block_kernel.astype(jnp.bfloat16))
    kernel = jnp.stack(kernel_list)
    back_table = jnp.exp(-decay_rates[None, None, :] * (closing_instant[:, None, :] - prefix_rows))
    start_table = mode_gains * jnp.exp(-decay_rates * prefix_rows)
    decays = jnp.exp(-decay_rates[None, :] * closing_instant)
    cur_blocks = currents.reshape(kernel_spans, KERNEL_SPAN, conductor_total)
    cot_blocks = seed_on_tension.reshape(kernel_spans, KERNEL_SPAN, conductor_total)
    local_fwd = jnp.einsum("bts,bsw->btw", kernel, cur_blocks, preferred_element_type=jnp.float32)
    fresh_fwd = jnp.einsum(
        "bsm,bsw->bmw",
        back_table.astype(jnp.bfloat16),
        cur_blocks,
        preferred_element_type=jnp.float32,
    )
    local_adj = jnp.einsum("bts,btw->bsw", kernel, cot_blocks, preferred_element_type=jnp.float32)
    fresh_adj = jnp.einsum(
        "btm,btw->bmw",
        start_table.astype(jnp.bfloat16),
        cot_blocks,
        preferred_element_type=jnp.float32,
    )
    dev_decay = jnp.ones((mode_count,), jnp.float32)
    resident_mode_values = jnp.zeros((mode_count, conductor_total), jnp.float32)
    for position in range(kernel_spans):
        dev_decay = dev_decay * decays[position]
        resident_mode_values = (
            decays[position][:, None] * resident_mode_values + fresh_fwd[position]
        )
    shard_adjoint_rows = jnp.zeros((mode_count, conductor_total), jnp.float32)
    for position in reversed(range(kernel_spans)):
        shard_adjoint_rows = decays[position][:, None] * shard_adjoint_rows + fresh_adj[position]
    no_decay = jnp.ones((mode_count,), jnp.float32)
    no_state = jnp.zeros((mode_count, conductor_total), jnp.float32)
    forward_pair = entering(
        (dev_decay, resident_mode_values), "tm", combine_states, (no_decay, no_state), False
    )
    adjoint_pair = entering(
        (dev_decay, shard_adjoint_rows), "tm", combine_states, (no_decay, no_state), True
    )
    state_in = forward_pair[1]
    adjoint_in = adjoint_pair[1]
    mode_state = state_in
    full_blocks = []
    for position in range(kernel_spans):
        carried_in = jnp.dot(
            start_table[position],
            mode_state,
            precision=lax.Precision.HIGHEST,
            preferred_element_type=jnp.float32,
        )
        full_blocks.append(length_scale[None, :] * (local_fwd[position] + carried_in))
        if position + 1 < kernel_spans:
            mode_state = decays[position][:, None] * mode_state + fresh_fwd[position]
    stress_full = jnp.stack(full_blocks)
    scores = SHARPNESS * stress_full
    local_high = jnp.max(scores, axis=(0, 1))
    highest = lax.pmax(local_high, "tm")
    amount = lax.psum(jnp.sum(jnp.exp(scores - highest), axis=(0, 1)), "tm")
    softened_peak_tension = (highest + jnp.log(amount)) / SHARPNESS
    adjoint_state = adjoint_in
    reversed_blocks = []
    for position in reversed(range(kernel_spans)):
        carried_in = jnp.dot(
            back_table[position],
            adjoint_state,
            precision=lax.Precision.HIGHEST,
            preferred_element_type=jnp.float32,
        )
        reversed_blocks.append(
            (length_scale[None, :] * (local_adj[position] + carried_in)).astype(jnp.bfloat16)
        )
        if position > 0:
            adjoint_state = decays[position][:, None] * adjoint_state + fresh_adj[position]
    gradient_wrt_draw = jnp.stack(reversed_blocks[::-1]).reshape(samples, conductor_total)
    tension_at_end = stress_full.astype(jnp.bfloat16).reshape(samples, conductor_total)
    return (tension_at_end, gradient_wrt_draw, softened_peak_tension)


def solution(mesh):
    placed = (P("tm", "parts"), P("tm", "parts"), P(None, ("parts", "tm")), P(), P(), P("parts"))
    return jax.shard_map(
        body,
        mesh=mesh,
        in_specs=placed,
        out_specs=(P("tm", "parts"), P("tm", "parts"), P("parts")),
        check_vma=False,
    )
```

profile of v0, /device:TPU:0, one launch (start us, length us, event | category | flops | bytes accessed | tf_op | source)
XLA Modules:
  0.0 303.3 jit_solution(5276616047635515305)
XLA Ops:
  7.2 0.0 copy-start
  7.2 0.0 all-gather.4.cloned.1.call-start
  7.2 2.1 reshape.270
  9.4 2.0 copy.54
  11.4 12.3 %reduce-window.6 = f32[32,4,6,128]{3,0,1,2:T(8,128)S(1)} reduce-window(f32[32,4,6,128]{3,0,1,2:T(8,128)} %copy.54, f32[]{:T(128)} %constant.65.clone.1), window={size=1x1x1x128 pad=0_0x0_0x0_0x127_0}, to_apply=%region_0.0 | reduce-window | flops 12484608 | bytes 786436 | tf_op jit(solution)/shard_map/reduce-window
  23.7 0.3 slice_reduce_fusion
  24.0 0.2 bitcast_bitcast_fusion.1
  24.2 0.2 slice_reduce_fusion.1
  24.4 0.7 fusion.53
  25.1 0.6 slice_bitcast_fusion.43
  25.7 0.2 fusion.40
  26.0 2.8 fusion.41
  28.8 0.0 copy-done.6
  28.8 0.6 fusion.43
  29.4 0.0 copy-start.14
  29.4 0.7 copy-done.14
  30.1 0.8 slice_add_fusion
  30.9 0.0 all-gather.4.cloned.1.call-update
  30.9 0.0 all-gather.6.cloned.1.call-start
  31.0 0.7 all-gather.6.cloned.1.call-update
  31.7 1.6 slice_bitcast_fusion.27
  33.3 0.1 fusion.54
  33.4 0.6 slice_negate_fusion.3
  34.0 0.2 iota_compare_fusion
  34.3 22.8 %multiply_reduce_fusion.15 = (f32[768,768]{1,0:T(8,128)}, f32[768,768]{1,0:T(8,128)}, f32[768,768]{1,0:T(8,128)}, f32[768,768]{1,0:T(8,128)}) fusion(f32[8,768]{1,0:T(8,128)S(1)} %get-tuple-element.194, f32[8]{0:T(128)S(1)} %get-tuple-element.210, f32[8]{0:T(128)S(1)} %get-tuple-element.206, pred[768,768]{1,0:T(8,128)(4,1)S(1)} %iota_compare_fusion, ...), kind=kLoop, calls=%fused_computation.19 | loop fusion | flops 92012544 | bytes 10125376 | tf_op jit(solution)/shard_map/reduce_sum | solution.py:54
  57.0 72.1 %multiply_reduce_fusion.14 = (f32[768,768]{1,0:T(8,128)}, f32[768,768]{1,0:T(8,128)}, f32[768,768]{1,0:T(8,128)}, f32[768,768]{1,0:T(8,128)}, f32[768,768]{1,0:T...) fusion(f32[8,768]{1,0:T(8,128)} %get-tuple-element.193, ...), kind=kLoop, calls=%fused_computation.18 | loop fusion | flops 276037632 | bytes 29196480 | tf_op jit(solution)/shard_map/reduce_sum | solution.py:54
  129.1 9.0 %fusion.28 = (bf16[1,768,768]{2,1,0:T(8,128)(2,1)}, bf16[1,768,768]{2,1,0:T(8,128)(2,1)}) fusion(f32[768,768]{1,0:T(8,128)} %get-tuple-element.156, f32[768,768]{1,0:T(8,128)} %get-tuple-element.152, f32[768,768]{1,0:T(8,128)} %get-tuple-element.137, f32[768,768]{1,0:T(8,128)} %get-tuple-element.133, f32[768,768]{1,0:T(8,128)} %get-tuple-element.155, ...), kind=kLoop, calls=%fused_computation.66 | loop fusion | flops 4718592 | bytes 21233664 | tf_op jit(solution)/shard_map/convert_element_type | solution.py:57
  138.1 7.1 %fusion.30 = (bf16[1,768,768]{2,1,0:T(8,128)(2,1)}, bf16[1,768,768]{2,1,0:T(8,128)(2,1)}) fusion(f32[768,768]{1,0:T(8,128)} %get-tuple-element.154, f32[768,768]{1,0:T(8,128)} %get-tuple-element.150, f32[768,768]{1,0:T(8,128)S(1)} %copy-done.11, f32[768,768]{1,0:T(8,128)S(1)} %copy-done.13, f32[768,768]{1,0:T(8,128)} %get-tuple-element.153, ...), kind=kLoop, calls=%fused_computation.68 | loop fusion | flops 4718592 | bytes 21233664 | tf_op jit(solution)/shard_map/convert_element_type | solution.py:57
  145.3 7.8 %fusion.34 = f32[4,768,512]{2,1,0:T(8,128)} fusion(bf16[4,768,512]{2,1,0:T(8,128)(2,1)S(1)} %bitcast.251, bf16[1,768,768]{2,1,0:T(8,128)(2,1)} %get-tuple-element.217, bf16[1,768,768]{2,1,0:T(8,128)(2,1)} %get-tuple-element.216, bf16[1,768,768]{2,1,0:T(8,128)(2,1)} %get-tuple-element.215, bf16[1,768,768]{2,1,0:T(8,128)(2,1)} %get-tuple-element.214), kind=kOutput, calls=%fused_computation.72 | convolution fusion | flops 2422996992 | bytes 14155776 | tf_op jit(solution)/shard_map/bts,bsw->btw/dot_general | solution.py:64
  153.1 4.8 %fusion.33 = f32[4,768,512]{2,1,0:T(8,128)} fusion(bf16[4,768,512]{2,1,0:T(8,128)(2,1)S(1)} %bitcast.255, bf16[1,768,768]{2,1,0:T(8,128)(2,1)S(1)} %copy-done.19, bf16[1,768,768]{2,1,0:T(8,128)(2,1)S(1)} %copy-done.18, bf16[1,768,768]{2,1,0:T(8,128)(2,1)S(1)} %copy-done.17, bf16[1,768,768]{2,1,0:T(8,128)(2,1)S(1)} %copy-done.16), kind=kOutput, calls=%fused_computation.71 | convolution fusion | flops 2422996992 | bytes 14155776 | tf_op jit(solution)/shard_map/bts,btw->bsw/dot_general | solution.py:71
  157.9 23.1 %all-gather = f32[16,1,32]{2,1,0:T(1,128)S(1)} all-gather(f32[1,1,32]{2,1,0:T(1,128)S(1)} %copy-done.28), channel_id=1, replica_groups=mesh['parts'=2,'tm'=16] {'tm'}, dimensions={0}, use_global_device_ids=true | all-gather | bytes 2176 | tf_op jit(solution)/shard_map/all_gather | solution.py:15
  181.1 4.3 %fusion.23 = f32[1,768,512]{2,1,0:T(8,128)} fusion(f32[4,768,512]{2,1,0:T(8,128)} %fusion.34, f32[32,512]{1,0:T(8,128)S(1)} %get-tuple-element.131, f32[512]{0:T(512)S(1)} %convert_multiply_fusion, f32[4,768,32]{1,2,0:T(8,128)} %copy-done.8), kind=kOutput, calls=%fused_computation.61 | convolution fusion | flops 151781376 | bytes 3311616 | tf_op jit(solution)/shard_map/dot_general | solution.py:101
  185.4 1.0 bitcast_add_fusion.8
  186.3 4.1 %fusion.17 = f32[1,768,512]{2,1,0:T(8,128)} fusion(f32[4,768,512]{2,1,0:T(8,128)} %fusion.34, f32[32,512]{1,0:T(8,128)S(1)} %bitcast_add_fusion.8, f32[512]{0:T(512)S(1)} %convert_multiply_fusion, f32[4,768,32]{1,2,0:T(8,128)} %copy-done.8), kind=kOutput, calls=%fused_computation.53 | convolution fusion | flops 151781376 | bytes 3311616 | tf_op jit(solution)/shard_map/dot_general | solution.py:101
  190.4 3.5 %fusion.20 = f32[1,768,512]{2,1,0:T(8,128)} fusion(f32[4,768,512]{2,1,0:T(8,128)S(1)} %copy-done.5, f32[512]{0:T(512)S(1)} %convert_multiply_fusion, f32[4,768,32]{1,2,0:T(8,128)S(1)} %copy-done.9, f32[32,512]{1,0:T(8,128)S(1)} %get-tuple-element.131, f32[4,32,512]{2,1,0:T(8,128)} %copy-done.14, f32[32]{0:T(128)S(1)} %copy-done.27), kind=kOutput, calls=%fused_computation.57 | convolution fusion | flops 151814144 | bytes 3377664 | tf_op jit(solution)/shard_map/dot_general | solution.py:101
  193.9 3.5 %fusion.14 = f32[1,768,512]{2,1,0:T(8,128)} fusion(f32[4,768,512]{2,1,0:T(8,128)S(1)} %copy-done.5, f32[512]{0:T(512)S(1)} %convert_multiply_fusion, f32[4,768,32]{1,2,0:T(8,128)S(1)} %copy-done.9, f32[32,512]{1,0:T(8,128)S(1)} %bitcast_add_fusion.8, f32[4,32,512]{2,1,0:T(8,128)} %copy-done.14, f32[32]{0:T(128)S(1)} %copy-done.25), kind=kOutput, calls=%fused_computation.49 | convolution fusion | flops 151814144 | bytes 3377664 | tf_op jit(solution)/shard_map/dot_general | solution.py:101
  197.3 14.0 %while.27 = (s32[]{:T(128)}, f32[32,512]{1,0:T(8,128)S(1)}, s32[]{:T(128)}, f32[16,32]{1,0:T(8,128)S(1)}, f32[16,32,512]{2,1,0:T(8,128)}, /*index=5*/s32[]{:T(128)}, s32[]{:T(128)}, s32[]{:T(128)}, s32[]{:T(128)}) while((s32[]{:T(128)}, f32[32,512]{1,0:T(8,128)S(1)}, s32[]{:T(128)}, f32[16,32]{1,0:T(8,128)S(1)}, f32[16,32,512]{2,1,0:T(8,128)}, ...), condition=%wide.region_21.22_spmd, body=%wide.region_20.21_spmd.sunk | while | flops 32774 | bytes 197139 | solution.py:24
  197.4 0.9 bitcast_add_fusion.15
  198.3 0.9 bitcast_add_fusion.15
  199.2 0.9 bitcast_add_fusion.15
  200.2 0.9 bitcast_add_fusion.15
  201.1 0.9 bitcast_add_fusion.15
  202.0 0.9 bitcast_add_fusion.15
  203.0 0.9 bitcast_add_fusion.15
  203.9 0.9 bitcast_add_fusion.15
  204.8 0.9 bitcast_add_fusion.15
  205.8 0.9 bitcast_add_fusion.15
  206.7 0.9 bitcast_add_fusion.15
  207.6 0.9 bitcast_add_fusion.15
  208.6 0.9 bitcast_add_fusion.15
  209.5 0.9 bitcast_add_fusion.15
  210.4 0.9 bitcast_add_fusion.15
  211.3 0.1 bitcast_add_fusion.4
  211.5 4.1 %fusion.24 = bf16[1,768,512]{2,1,0:T(8,128)(2,1)} fusion(f32[4,768,512]{2,1,0:T(8,128)} %fusion.33, f32[512]{0:T(512)S(1)} %convert_multiply_fusion, f32[4,768,32]{1,2,0:T(8,128)} %copy-done.6, f32[32,512]{1,0:T(8,128)S(1)} %bitcast_add_fusion.4, f32[4,32,512]{2,1,0:T(8,128)S(1)} %fusion.41, f32[32]{0:T(128)S(1)} %copy-done.23), kind=kOutput, calls=%fused_computation.62 | convolution fusion | flops 152207360 | bytes 2591232 | tf_op jit(solution)/shard_map/dot_general | solution.py:119
  215.5 3.9 %fusion.25 = bf16[1,768,512]{2,1,0:T(8,128)(2,1)} fusion(f32[32,512]{1,0:T(8,128)S(1)} %bitcast_add_fusion.4, f32[4,768,512]{2,1,0:T(8,128)} %fusion.33, f32[512]{0:T(512)S(1)} %convert_multiply_fusion, f32[4,768,32]{1,2,0:T(8,128)} %copy-done.6), kind=kOutput, calls=%fused_computation.63 | convolution fusion | flops 152174592 | bytes 2525184 | tf_op jit(solution)/shard_map/dot_general | solution.py:119
  219.4 3.8 %fusion.26 = bf16[1,768,512]{2,1,0:T(8,128)(2,1)} fusion(f32[4,768,512]{2,1,0:T(8,128)} %fusion.33, f32[512]{0:T(512)S(1)} %convert_multiply_fusion, f32[4,768,32]{1,2,0:T(8,128)S(1)} %copy-done.7, f32[32,512]{1,0:T(8,128)S(1)} %get-tuple-element.132, f32[4,32,512]{2,1,0:T(8,128)S(1)} %fusion.41, f32[32]{0:T(128)S(1)} %get-tuple-element.198), kind=kOutput, calls=%fused_computation.64 | convolution fusion | flops 152207360 | bytes 2591232 | tf_op jit(solution)/shard_map/dot_general | solution.py:119
  223.2 3.8 %fusion.27 = bf16[1,768,512]{2,1,0:T(8,128)(2,1)} fusion(f32[32,512]{1,0:T(8,128)S(1)} %get-tuple-element.132, f32[4,768,512]{2,1,0:T(8,128)} %fusion.33, f32[512]{0:T(512)S(1)} %convert_multiply_fusion, f32[4,768,32]{1,2,0:T(8,128)S(1)} %copy-done.7), kind=kOutput, calls=%fused_computation.65 | convolution fusion | flops 152174592 | bytes 2525184 | tf_op jit(solution)/shard_map/dot_general | solution.py:119
  227.0 0.9 multiply_reduce_fusion.16
  227.9 2.1 fusion.32
  229.9 29.8 %pmax.7 = f32[512]{0:T(512)S(1)} all-reduce(f32[512]{0:T(512)S(1)} %multiply_reduce_fusion.16), channel_id=1, replica_groups=mesh['parts'=2,'tm'=16] {'tm'}, use_global_device_ids=true, to_apply=%region_23.24 | all-reduce | flops 512 | bytes 4096 | tf_op jit(solution)/shard_map/pmax | solution.py:113
  259.7 3.4 %exponential_reduce_fusion = f32[512]{0:T(512)S(1)} fusion(f32[512]{0:T(512)S(1)} %pmax.7, f32[1,768,512]{2,1,0:T(8,128)} %fusion.14, f32[1,768,512]{2,1,0:T(8,128)} %fusion.17, f32[1,768,512]{2,1,0:T(8,128)} %fusion.20, f32[1,768,512]{2,1,0:T(8,128)} %fusion.23), kind=kLoop, calls=%fused_computation.21 | loop fusion | flops 9436672 | bytes 6295552 | tf_op jit(solution)/shard_map/reduce_sum | solution.py:114
  263.1 29.5 %psum.7 = f32[512]{0:T(512)S(1)} all-reduce(f32[512]{0:T(512)S(1)} %exponential_reduce_fusion), channel_id=1, replica_groups=mesh['parts'=2,'tm'=16] {'tm'}, use_global_device_ids=true, to_apply=%region_25.26 | all-reduce | flops 512 | bytes 4096 | tf_op jit(solution)/shard_map/psum | solution.py:114
  292.6 0.6 add_multiply_fusion
  293.2 3.2 %pad_maximum_fusion.2 = bf16[4,768,512]{2,1,0:T(8,128)(2,1)} fusion(bf16[1,768,512]{2,1,0:T(8,128)(2,1)} %fusion.27, bf16[1,768,512]{2,1,0:T(8,128)(2,1)} %fusion.26, bf16[1,768,512]{2,1,0:T(8,128)(2,1)} %fusion.25, bf16[1,768,512]{2,1,0:T(8,128)(2,1)} %fusion.24), kind=kLoop, calls=%fused_computation.24 | loop fusion | flops 4718592 | bytes 6291456 | tf_op jit(solution)/shard_map/stack | solution.py:130
  (83 shorter events, 0.3 us)
Async XLA Ops:
  7.2 21.6 %copy-start = (bf16[3072,512]{1,0:T(8,128)(2,1)S(1)}, bf16[3072,512]{1,0:T(8,128)(2,1)}, u32[]{:S(2)}) copy-start(bf16[3072,512]{1,0:T(8,128)(2,1)} %param.10) | copy-start | bytes 9437188
  7.2 173.9 %all-gather.4.cloned.1.call-start = ((), (), s32[]{:S(2)}) async-start(), calls=%async_computation | async-start | bytes 1114112 | tf_op jit(solution)/shard_map/all_gather | solution.py:15
  24.2 1.7 copy-start.15
  25.7 5.2 %copy-start.22 = (f32[32]{0:T(128)}, f32[32]{0:T(128)S(1)}, u32[]{:S(2)}) copy-start(f32[32]{0:T(128)S(1)} %get-tuple-element.201) | copy-start | bytes 388
  25.7 5.2 %copy-start.24 = (f32[32]{0:T(128)}, f32[32]{0:T(128)S(1)}, u32[]{:S(2)}) copy-start(f32[32]{0:T(128)S(1)} %get-tuple-element.200) | copy-start | bytes 388
  25.7 5.2 %copy-start.26 = (f32[32]{0:T(128)}, f32[32]{0:T(128)S(1)}, u32[]{:S(2)}) copy-start(f32[32]{0:T(128)S(1)} %get-tuple-element.197) | copy-start | bytes 388
  25.9 2.9 copy-start.6
  25.9 3.5 %copy-start.8 = (f32[4,768,32]{1,2,0:T(8,128)}, f32[4,768,32]{1,2,0:T(8,128)S(1)}, u32[]{:S(2)}) copy-start(f32[4,768,32]{1,2,0:T(8,128)S(1)} %get-tuple-element.178) | copy-start | bytes 1179652
  25.9 7.5 %copy-start.21 = (f32[32]{0:T(128)S(1)}, f32[32]{0:T(128)}, u32[]{:S(2)}) copy-start(f32[32]{0:T(128)} %param.13) | copy-start | bytes 388
  29.4 0.7 copy-start.14
  30.9 166.4 %all-gather.6.cloned.1.call-start = ((), (), s32[]{:S(2)}) async-start(), calls=%async_computation.1 | async-start | bytes 1114112 | tf_op jit(solution)/shard_map/all_gather | solution.py:15
  34.2 22.8 %copy-start.20 = (pred[768,768]{1,0:T(8,128)(4,1)}, pred[768,768]{1,0:T(8,128)(4,1)S(1)}, u32[]{:S(2)}) copy-start(pred[768,768]{1,0:T(8,128)(4,1)S(1)} %iota_compare_fusion) | copy-start | bytes 1769476
  34.2 22.8 %copy-start.30 = (f32[8]{0:T(128)S(1)}, f32[8]{0:T(128)}, u32[]{:S(2)}) copy-start(f32[8]{0:T(128)} %get-tuple-element.212) | copy-start | bytes 100
  129.1 9.0 %copy-start.11 = (f32[768,768]{1,0:T(8,128)S(1)}, f32[768,768]{1,0:T(8,128)}, u32[]{:S(2)}) copy-start(f32[768,768]{1,0:T(8,128)} %get-tuple-element.139) | copy-start | bytes 7077892
  129.1 9.0 %copy-start.12 = (f32[768,768]{1,0:T(8,128)S(1)}, f32[768,768]{1,0:T(8,128)}, u32[]{:S(2)}) copy-start(f32[768,768]{1,0:T(8,128)} %get-tuple-element.140) | copy-start | bytes 7077892
  129.1 9.0 %copy-start.13 = (f32[768,768]{1,0:T(8,128)S(1)}, f32[768,768]{1,0:T(8,128)}, u32[]{:S(2)}) copy-start(f32[768,768]{1,0:T(8,128)} %get-tuple-element.135) | copy-start | bytes 7077892
  145.2 7.8 %copy-start.10 = (bf16[3072,512]{1,0:T(8,128)(2,1)S(1)}, bf16[3072,512]{1,0:T(8,128)(2,1)}, u32[]{:S(2)}) copy-start(bf16[3072,512]{1,0:T(8,128)(2,1)} %param.11) | copy-start | bytes 9437188
  145.2 7.8 %copy-start.16 = (bf16[1,768,768]{2,1,0:T(8,128)(2,1)S(1)}, bf16[1,768,768]{2,1,0:T(8,128)(2,1)}, u32[]{:S(2)}) copy-start(bf16[1,768,768]{2,1,0:T(8,128)(2,1)} %get-tuple-element.214) | copy-start | bytes 3538948
  145.2 7.8 %copy-start.17 = (bf16[1,768,768]{2,1,0:T(8,128)(2,1)S(1)}, bf16[1,768,768]{2,1,0:T(8,128)(2,1)}, u32[]{:S(2)}) copy-start(bf16[1,768,768]{2,1,0:T(8,128)(2,1)} %get-tuple-element.215) | copy-start | bytes 3538948
  145.2 7.8 %copy-start.18 = (bf16[1,768,768]{2,1,0:T(8,128)(2,1)S(1)}, bf16[1,768,768]{2,1,0:T(8,128)(2,1)}, u32[]{:S(2)}) copy-start(bf16[1,768,768]{2,1,0:T(8,128)(2,1)} %get-tuple-element.216) | copy-start | bytes 3538948
  145.3 7.8 %copy-start.19 = (bf16[1,768,768]{2,1,0:T(8,128)(2,1)S(1)}, bf16[1,768,768]{2,1,0:T(8,128)(2,1)}, u32[]{:S(2)}) copy-start(bf16[1,768,768]{2,1,0:T(8,128)(2,1)} %get-tuple-element.217) | copy-start | bytes 3538948
  153.1 4.9 %copy-start.28 = (f32[1,1,32]{2,1,0:T(1,128)S(1)}, f32[1,1,32]{2,1,0:T(1,128)}, u32[]{:S(2)}) copy-start(f32[1,1,32]{2,1,0:T(1,128)} %get-tuple-element.199) | copy-start | bytes 388
  153.1 28.0 %copy-start.29 = (s32[512]{0:T(512)S(1)}, s32[512]{0:T(512)}, u32[]{:S(2)}) copy-start(s32[512]{0:T(512)} %param.15) | copy-start | bytes 6148
  153.1 32.3 %copy-start.23 = (f32[32]{0:T(128)S(1)}, f32[32]{0:T(128)}, u32[]{:S(2)}) copy-start(f32[32]{0:T(128)} %copy-done.22) | copy-start | bytes 388
  153.1 32.3 %copy-start.27 = (f32[32]{0:T(128)S(1)}, f32[32]{0:T(128)}, u32[]{:S(2)}) copy-start(f32[32]{0:T(128)} %copy-done.26) | copy-start | bytes 388
  181.1 9.3 %copy-start.5 = (f32[4,768,512]{2,1,0:T(8,128)S(1)}, f32[4,768,512]{2,1,0:T(8,128)}, u32[]{:S(2)}) copy-start(f32[4,768,512]{2,1,0:T(8,128)} %fusion.34) | copy-start | bytes 18874372
  181.1 9.3 %copy-start.9 = (f32[4,768,32]{1,2,0:T(8,128)S(1)}, f32[4,768,32]{1,2,0:T(8,128)}, u32[]{:S(2)}) copy-start(f32[4,768,32]{1,2,0:T(8,128)} %copy-done.8) | copy-start | bytes 1179652
  181.1 12.8 %copy-start.25 = (f32[32]{0:T(128)S(1)}, f32[32]{0:T(128)}, u32[]{:S(2)}) copy-start(f32[32]{0:T(128)} %copy-done.24) | copy-start | bytes 388
  211.3 8.1 %copy-start.7 = (f32[4,768,32]{1,2,0:T(8,128)S(1)}, f32[4,768,32]{1,2,0:T(8,128)}, u32[]{:S(2)}) copy-start(f32[4,768,32]{1,2,0:T(8,128)} %copy-done.6) | copy-start | bytes 1179652
  211.4 15.6 %copy-start.1 = (f32[1,768,512]{2,1,0:T(8,128)S(1)}, f32[1,768,512]{2,1,0:T(8,128)}, u32[]{:S(2)}) copy-start(f32[1,768,512]{2,1,0:T(8,128)} %fusion.23) | copy-start | bytes 4718596
  211.4 15.6 %copy-start.2 = (f32[1,768,512]{2,1,0:T(8,128)S(1)}, f32[1,768,512]{2,1,0:T(8,128)}, u32[]{:S(2)}) copy-start(f32[1,768,512]{2,1,0:T(8,128)} %fusion.17) | copy-start | bytes 4718596
  211.5 15.6 %copy-start.3 = (f32[1,768,512]{2,1,0:T(8,128)S(1)}, f32[1,768,512]{2,1,0:T(8,128)}, u32[]{:S(2)}) copy-start(f32[1,768,512]{2,1,0:T(8,128)} %fusion.20) | copy-start | bytes 4718596
  211.5 15.5 %copy-start.4 = (f32[1,768,512]{2,1,0:T(8,128)S(1)}, f32[1,768,512]{2,1,0:T(8,128)}, u32[]{:S(2)}) copy-start(f32[1,768,512]{2,1,0:T(8,128)} %fusion.14) | copy-start | bytes 4718596
Sparse Core Ops, SparseCore 0:
  31.1 40.6 all-gather.3
  73.9 36.8 all-gather.5
where the time goes:
time: 305 us; the launch traced here: 303 us
  other arithmetic  152 us (50%)
  blocking collectives  82.4 us (27%)
  matrix products  46.8 us (15%)
  between operations  14.4 us (5%)
  local copies, waits for them, and re-layouts  7.32 us (2%)
    reduce_sum x2, other arithmetic, body(): jnp.sum(gain_part[:, None, None] * jnp.exp(-rate_part[:, None, None] * sp...  94.9 us
    pmax x1, blocking collectives, body(): highest = lax.pmax(local_high, 'tm')  29.8 us
    psum x1, blocking collectives, body(): amount = lax.psum(jnp.sum(jnp.exp(scores - highest), axis=(0, 1)), 'tm')  29.5 us
    all_gather x1, blocking collectives, entering(): gathered = jax.tree.map(lambda a: lax.all_gather(a, axis), part)  23.1 us
    convert_element_type x2, other arithmetic, body(): kernel_list.append(block_kernel.astype(jnp.bfloat16))  16.1 us
    dot_general x4, matrix products, body(): jnp.dot(back_table[position], adjoint_state, precision=lax.Precision.HIGH...  15.5 us
    dot_general x4, matrix products, body(): jnp.dot(start_table[position], mode_state, precision=lax.Precision.HIGHES...  15.2 us
    add x15, other arithmetic, combine_states(): return (earlier[0] * latter[0], latter[0][:, None] * earlier[1] + latter[1])  13.8 us
  transfers between devices with their start and end apart: 2, of which 0 were waited for; matrix products, arithmetic and copies ran while one was open for 47% of the time, Pallas kernels for 0%

commit v1 on v0

--- a/solution.py
+++ b/solution.py
@@ -111,7 +111,9 @@
     scores = SHARPNESS * stress_full
     local_high = jnp.max(scores, axis=(0, 1))
     highest = lax.pmax(local_high, "tm")
-    amount = lax.psum(jnp.sum(jnp.exp(scores - highest), axis=(0, 1)), "tm")
+    block = jnp.sum(jnp.exp(scores - highest), axis=(0, 1))
+    shards = lax.all_gather(block, "tm", axis=0, tiled=False)
+    amount = shards.sum(axis=0)
     softened_peak_tension = (highest + jnp.log(amount)) / SHARPNESS
     adjoint_state = adjoint_in
     reversed_blocks = []

time: 305 us -> 293 us (0.961)
  blocking collectives: 82.4 us -> 70.1 us
    psum x1 -> x0, blocking collectives: 29.5 us -> none  [body(): amount = lax.psum(jnp.sum(jnp.exp(scores - highest), axis=(0, 1)), 'tm')]
    all_gather x0 -> x1, blocking collectives: none -> 17.2 us  [body(): shards = lax.all_gather(block, 'tm', axis=0, tiled=False)]
  transfers between devices with their start and end apart: 2 -> 2, of which waited for: 0 -> 0; matrix products, arithmetic and copies ran while one was open for 47% -> 49% of each run, Pallas kernels for 0% -> 0%
where the time goes in v1:
time: 293 us; the launch traced here: 291 us
  other arithmetic  152 us (52%)
  blocking collectives  70.1 us (24%)
  matrix products  46.8 us (16%)
  between operations  14.4 us (5%)
  local copies, waits for them, and re-layouts  7.32 us (2%)
    reduce_sum x2, other arithmetic, body(): jnp.sum(gain_part[:, None, None] * jnp.exp(-rate_part[:, None, None] * sp...  94.9 us
    pmax x1, blocking collectives, body(): highest = lax.pmax(local_high, 'tm')  29.8 us
    all_gather x1, blocking collectives, entering(): gathered = jax.tree.map(lambda a: lax.all_gather(a, axis), part)  23.1 us
    all_gather x1, blocking collectives, body(): shards = lax.all_gather(block, 'tm', axis=0, tiled=False)  17.2 us
    convert_element_type x2, other arithmetic, body(): kernel_list.append(block_kernel.astype(jnp.bfloat16))  16.1 us
    dot_general x4, matrix products, body(): jnp.dot(back_table[position], adjoint_state, precision=lax.Precision.HIGH...  15.5 us
    dot_general x4, matrix products, body(): jnp.dot(start_table[position], mode_state, precision=lax.Precision.HIGHES...  15.2 us
    add x15, other arithmetic, combine_states(): return (earlier[0] * latter[0], latter[0][:, None] * earlier[1] + latter[1])  13.8 us
  transfers between devices with their start and end apart: 2, of which 0 were waited for; matrix products, arithmetic and copies ran while one was open for 49% of the time, Pallas kernels for 0%

profile of v1, /device:TPU:0, one launch (start us, length us, event | category | flops | bytes accessed | tf_op | source)
XLA Modules:
  0.0 291.0 jit_solution(3093160504681461550)
XLA Ops:
  7.2 0.0 copy-start
  7.2 0.0 all-gather.6.cloned.1.call-start
  7.2 2.1 reshape.270
  9.4 2.0 copy.54
  11.4 12.3 %reduce-window.6 = f32[32,4,6,128]{3,0,1,2:T(8,128)S(1)} reduce-window(f32[32,4,6,128]{3,0,1,2:T(8,128)} %copy.54, f32[]{:T(128)} %constant.65.clone.1), window={size=1x1x1x128 pad=0_0x0_0x0_0x127_0}, to_apply=%region_0.0 | reduce-window | flops 12484608 | bytes 786436 | tf_op jit(solution)/shard_map/reduce-window
  23.7 0.3 slice_reduce_fusion
  24.0 0.2 bitcast_bitcast_fusion.1
  24.2 0.2 slice_reduce_fusion.1
  24.4 0.7 fusion.53
  25.1 0.6 slice_bitcast_fusion.43
  25.7 0.2 fusion.40
  26.0 2.8 fusion.41
  28.8 0.0 copy-done.6
  28.8 0.6 fusion.43
  29.4 0.0 copy-start.14
  29.4 0.7 copy-done.14
  30.1 0.8 slice_add_fusion
  30.9 0.0 all-gather.6.cloned.1.call-update
  30.9 0.0 all-gather.8.cloned.1.call-start
  31.0 0.7 all-gather.8.cloned.1.call-update
  31.7 1.6 slice_bitcast_fusion.27
  33.3 0.1 fusion.54
  33.4 0.6 slice_negate_fusion.3
  34.0 0.2 iota_compare_fusion
  34.3 22.8 %multiply_reduce_fusion.15 = (f32[768,768]{1,0:T(8,128)}, f32[768,768]{1,0:T(8,128)}, f32[768,768]{1,0:T(8,128)}, f32[768,768]{1,0:T(8,128)}) fusion(f32[8,768]{1,0:T(8,128)S(1)} %get-tuple-element.194, f32[8]{0:T(128)S(1)} %get-tuple-element.210, f32[8]{0:T(128)S(1)} %get-tuple-element.206, pred[768,768]{1,0:T(8,128)(4,1)S(1)} %iota_compare_fusion, ...), kind=kLoop, calls=%fused_computation.19 | loop fusion | flops 92012544 | bytes 10125376 | tf_op jit(solution)/shard_map/reduce_sum | solution.py:54
  57.0 72.1 %multiply_reduce_fusion.14 = (f32[768,768]{1,0:T(8,128)}, f32[768,768]{1,0:T(8,128)}, f32[768,768]{1,0:T(8,128)}, f32[768,768]{1,0:T(8,128)}, f32[768,768]{1,0:T...) fusion(f32[8,768]{1,0:T(8,128)} %get-tuple-element.193, ...), kind=kLoop, calls=%fused_computation.18 | loop fusion | flops 276037632 | bytes 29196480 | tf_op jit(solution)/shard_map/reduce_sum | solution.py:54
  129.1 9.0 %fusion.28 = (bf16[1,768,768]{2,1,0:T(8,128)(2,1)}, bf16[1,768,768]{2,1,0:T(8,128)(2,1)}) fusion(f32[768,768]{1,0:T(8,128)} %get-tuple-element.156, f32[768,768]{1,0:T(8,128)} %get-tuple-element.152, f32[768,768]{1,0:T(8,128)} %get-tuple-element.137, f32[768,768]{1,0:T(8,128)} %get-tuple-element.133, f32[768,768]{1,0:T(8,128)} %get-tuple-element.155, ...), kind=kLoop, calls=%fused_computation.66 | loop fusion | flops 4718592 | bytes 21233664 | tf_op jit(solution)/shard_map/convert_element_type | solution.py:57
  138.1 7.1 %fusion.30 = (bf16[1,768,768]{2,1,0:T(8,128)(2,1)}, bf16[1,768,768]{2,1,0:T(8,128)(2,1)}) fusion(f32[768,768]{1,0:T(8,128)} %get-tuple-element.154, f32[768,768]{1,0:T(8,128)} %get-tuple-element.150, f32[768,768]{1,0:T(8,128)S(1)} %copy-done.11, f32[768,768]{1,0:T(8,128)S(1)} %copy-done.13, f32[768,768]{1,0:T(8,128)} %get-tuple-element.153, ...), kind=kLoop, calls=%fused_computation.68 | loop fusion | flops 4718592 | bytes 21233664 | tf_op jit(solution)/shard_map/convert_element_type | solution.py:57
  145.3 7.8 %fusion.34 = f32[4,768,512]{2,1,0:T(8,128)} fusion(bf16[4,768,512]{2,1,0:T(8,128)(2,1)S(1)} %bitcast.252, bf16[1,768,768]{2,1,0:T(8,128)(2,1)} %get-tuple-element.217, bf16[1,768,768]{2,1,0:T(8,128)(2,1)} %get-tuple-element.216, bf16[1,768,768]{2,1,0:T(8,128)(2,1)} %get-tuple-element.215, bf16[1,768,768]{2,1,0:T(8,128)(2,1)} %get-tuple-element.214), kind=kOutput, calls=%fused_computation.72 | convolution fusion | flops 2422996992 | bytes 14155776 | tf_op jit(solution)/shard_map/bts,bsw->btw/dot_general | solution.py:64
  153.1 4.8 %fusion.33 = f32[4,768,512]{2,1,0:T(8,128)} fusion(bf16[4,768,512]{2,1,0:T(8,128)(2,1)S(1)} %bitcast.256, bf16[1,768,768]{2,1,0:T(8,128)(2,1)S(1)} %copy-done.19, bf16[1,768,768]{2,1,0:T(8,128)(2,1)S(1)} %copy-done.18, bf16[1,768,768]{2,1,0:T(8,128)(2,1)S(1)} %copy-done.17, bf16[1,768,768]{2,1,0:T(8,128)(2,1)S(1)} %copy-done.16), kind=kOutput, calls=%fused_computation.71 | convolution fusion | flops 2422996992 | bytes 14155776 | tf_op jit(solution)/shard_map/bts,btw->bsw/dot_general | solution.py:71
  157.9 23.1 %all-gather.1 = f32[16,1,32]{2,1,0:T(1,128)S(1)} all-gather(f32[1,1,32]{2,1,0:T(1,128)S(1)} %copy-done.28), channel_id=1, replica_groups=mesh['parts'=2,'tm'=16] {'tm'}, dimensions={0}, use_global_device_ids=true | all-gather | bytes 2176 | tf_op jit(solution)/shard_map/all_gather | solution.py:15
  181.1 4.3 %fusion.23 = f32[1,768,512]{2,1,0:T(8,128)} fusion(f32[4,768,512]{2,1,0:T(8,128)} %fusion.34, f32[32,512]{1,0:T(8,128)S(1)} %get-tuple-element.131, f32[512]{0:T(512)S(1)} %convert_multiply_fusion, f32[4,768,32]{1,2,0:T(8,128)} %copy-done.8), kind=kOutput, calls=%fused_computation.61 | convolution fusion | flops 151781376 | bytes 3311616 | tf_op jit(solution)/shard_map/dot_general | solution.py:101
  185.4 1.0 bitcast_add_fusion.8
  186.3 4.1 %fusion.17 = f32[1,768,512]{2,1,0:T(8,128)} fusion(f32[4,768,512]{2,1,0:T(8,128)} %fusion.34, f32[32,512]{1,0:T(8,128)S(1)} %bitcast_add_fusion.8, f32[512]{0:T(512)S(1)} %convert_multiply_fusion, f32[4,768,32]{1,2,0:T(8,128)} %copy-done.8), kind=kOutput, calls=%fused_computation.53 | convolution fusion | flops 151781376 | bytes 3311616 | tf_op jit(solution)/shard_map/dot_general | solution.py:101
  190.4 3.5 %fusion.20 = f32[1,768,512]{2,1,0:T(8,128)} fusion(f32[4,768,512]{2,1,0:T(8,128)S(1)} %copy-done.5, f32[512]{0:T(512)S(1)} %convert_multiply_fusion, f32[4,768,32]{1,2,0:T(8,128)S(1)} %copy-done.9, f32[32,512]{1,0:T(8,128)S(1)} %get-tuple-element.131, f32[4,32,512]{2,1,0:T(8,128)} %copy-done.14, f32[32]{0:T(128)S(1)} %copy-done.27), kind=kOutput, calls=%fused_computation.57 | convolution fusion | flops 151814144 | bytes 3377664 | tf_op jit(solution)/shard_map/dot_general | solution.py:101
  193.9 3.5 %fusion.14 = f32[1,768,512]{2,1,0:T(8,128)} fusion(f32[4,768,512]{2,1,0:T(8,128)S(1)} %copy-done.5, f32[512]{0:T(512)S(1)} %convert_multiply_fusion, f32[4,768,32]{1,2,0:T(8,128)S(1)} %copy-done.9, f32[32,512]{1,0:T(8,128)S(1)} %bitcast_add_fusion.8, f32[4,32,512]{2,1,0:T(8,128)} %copy-done.14, f32[32]{0:T(128)S(1)} %copy-done.25), kind=kOutput, calls=%fused_computation.49 | convolution fusion | flops 151814144 | bytes 3377664 | tf_op jit(solution)/shard_map/dot_general | solution.py:101
  197.3 14.0 %while.27 = (s32[]{:T(128)}, f32[32,512]{1,0:T(8,128)S(1)}, s32[]{:T(128)}, f32[16,32]{1,0:T(8,128)S(1)}, f32[16,32,512]{2,1,0:T(8,128)}, /*index=5*/s32[]{:T(128)}, s32[]{:T(128)}, s32[]{:T(128)}, s32[]{:T(128)}) while((s32[]{:T(128)}, f32[32,512]{1,0:T(8,128)S(1)}, s32[]{:T(128)}, f32[16,32]{1,0:T(8,128)S(1)}, f32[16,32,512]{2,1,0:T(8,128)}, ...), condition=%wide.region_21.22_spmd, body=%wide.region_20.21_spmd.sunk | while | flops 32774 | bytes 197139 | solution.py:24
  197.4 0.9 bitcast_add_fusion.15
  198.3 0.9 bitcast_add_fusion.15
  199.2 0.9 bitcast_add_fusion.15
  200.2 0.9 bitcast_add_fusion.15
  201.1 0.9 bitcast_add_fusion.15
  202.0 0.9 bitcast_add_fusion.15
  203.0 0.9 bitcast_add_fusion.15
  203.9 0.9 bitcast_add_fusion.15
  204.8 0.9 bitcast_add_fusion.15
  205.8 0.9 bitcast_add_fusion.15
  206.7 0.9 bitcast_add_fusion.15
  207.6 0.9 bitcast_add_fusion.15
  208.6 0.9 bitcast_add_fusion.15
  209.5 0.9 bitcast_add_fusion.15
  210.4 0.9 bitcast_add_fusion.15
  211.3 0.1 bitcast_add_fusion.4
  211.5 4.1 %fusion.24 = bf16[1,768,512]{2,1,0:T(8,128)(2,1)} fusion(f32[4,768,512]{2,1,0:T(8,128)} %fusion.33, f32[512]{0:T(512)S(1)} %convert_multiply_fusion, f32[4,768,32]{1,2,0:T(8,128)} %copy-done.6, f32[32,512]{1,0:T(8,128)S(1)} %bitcast_add_fusion.4, f32[4,32,512]{2,1,0:T(8,128)S(1)} %fusion.41, f32[32]{0:T(128)S(1)} %copy-done.23), kind=kOutput, calls=%fused_computation.62 | convolution fusion | flops 152207360 | bytes 2591232 | tf_op jit(solution)/shard_map/dot_general | solution.py:121
  215.5 3.9 %fusion.25 = bf16[1,768,512]{2,1,0:T(8,128)(2,1)} fusion(f32[32,512]{1,0:T(8,128)S(1)} %bitcast_add_fusion.4, f32[4,768,512]{2,1,0:T(8,128)} %fusion.33, f32[512]{0:T(512)S(1)} %convert_multiply_fusion, f32[4,768,32]{1,2,0:T(8,128)} %copy-done.6), kind=kOutput, calls=%fused_computation.63 | convolution fusion | flops 152174592 | bytes 2525184 | tf_op jit(solution)/shard_map/dot_general | solution.py:121
  219.4 3.8 %fusion.26 = bf16[1,768,512]{2,1,0:T(8,128)(2,1)} fusion(f32[4,768,512]{2,1,0:T(8,128)} %fusion.33, f32[512]{0:T(512)S(1)} %convert_multiply_fusion, f32[4,768,32]{1,2,0:T(8,128)S(1)} %copy-done.7, f32[32,512]{1,0:T(8,128)S(1)} %get-tuple-element.132, f32[4,32,512]{2,1,0:T(8,128)S(1)} %fusion.41, f32[32]{0:T(128)S(1)} %get-tuple-element.198), kind=kOutput, calls=%fused_computation.64 | convolution fusion | flops 152207360 | bytes 2591232 | tf_op jit(solution)/shard_map/dot_general | solution.py:121
  223.2 3.8 %fusion.27 = bf16[1,768,512]{2,1,0:T(8,128)(2,1)} fusion(f32[32,512]{1,0:T(8,128)S(1)} %get-tuple-element.132, f32[4,768,512]{2,1,0:T(8,128)} %fusion.33, f32[512]{0:T(512)S(1)} %convert_multiply_fusion, f32[4,768,32]{1,2,0:T(8,128)S(1)} %copy-done.7), kind=kOutput, calls=%fused_computation.65 | convolution fusion | flops 152174592 | bytes 2525184 | tf_op jit(solution)/shard_map/dot_general | solution.py:121
  227.0 0.9 multiply_reduce_fusion.16
  227.9 2.1 fusion.32
  229.9 29.8 %pmax.7 = f32[512]{0:T(512)S(1)} all-reduce(f32[512]{0:T(512)S(1)} %multiply_reduce_fusion.16), channel_id=1, replica_groups=mesh['parts'=2,'tm'=16] {'tm'}, use_global_device_ids=true, to_apply=%region_23.24 | all-reduce | flops 512 | bytes 4096 | tf_op jit(solution)/shard_map/pmax | solution.py:113
  259.7 3.4 %exponential_reduce_fusion = f32[512]{0:T(512)S(1)} fusion(f32[512]{0:T(512)S(1)} %pmax.7, f32[1,768,512]{2,1,0:T(8,128)} %fusion.14, f32[1,768,512]{2,1,0:T(8,128)} %fusion.17, f32[1,768,512]{2,1,0:T(8,128)} %fusion.20, f32[1,768,512]{2,1,0:T(8,128)} %fusion.23), kind=kLoop, calls=%fused_computation.21 | loop fusion | flops 9436672 | bytes 6295552 | tf_op jit(solution)/shard_map/reduce_sum | solution.py:114
  263.1 17.2 %all-gather.2 = f32[16,1,512]{2,1,0:T(1,128)S(1)} all-gather(f32[1,1,512]{2,1,0:T(1,128)S(1)} %bitcast.258), channel_id=2, replica_groups=mesh['parts'=2,'tm'=16] {'tm'}, dimensions={0}, use_global_device_ids=true | all-gather | bytes 34816 | tf_op jit(solution)/shard_map/all_gather | solution.py:115
  280.4 0.6 add_multiply_fusion
  281.0 3.2 %pad_maximum_fusion.2 = bf16[4,768,512]{2,1,0:T(8,128)(2,1)} fusion(bf16[1,768,512]{2,1,0:T(8,128)(2,1)} %fusion.27, bf16[1,768,512]{2,1,0:T(8,128)(2,1)} %fusion.26, bf16[1,768,512]{2,1,0:T(8,128)(2,1)} %fusion.25, bf16[1,768,512]{2,1,0:T(8,128)(2,1)} %fusion.24), kind=kLoop, calls=%fused_computation.24 | loop fusion | flops 4718592 | bytes 6291456 | tf_op jit(solution)/shard_map/stack | solution.py:132
  (84 shorter events, 0.3 us)
Async XLA Ops:
  7.2 21.6 %copy-start = (bf16[3072,512]{1,0:T(8,128)(2,1)S(1)}, bf16[3072,512]{1,0:T(8,128)(2,1)}, u32[]{:S(2)}) copy-start(bf16[3072,512]{1,0:T(8,128)(2,1)} %param.10) | copy-start | bytes 9437188
  7.2 173.9 %all-gather.6.cloned.1.call-start = ((), (), s32[]{:S(2)}) async-start(), calls=%async_computation | async-start | bytes 1114112 | tf_op jit(solution)/shard_map/all_gather | solution.py:15
  24.2 1.7 copy-start.15
  25.7 5.2 %copy-start.22 = (f32[32]{0:T(128)}, f32[32]{0:T(128)S(1)}, u32[]{:S(2)}) copy-start(f32[32]{0:T(128)S(1)} %get-tuple-element.201) | copy-start | bytes 388
  25.7 5.2 %copy-start.24 = (f32[32]{0:T(128)}, f32[32]{0:T(128)S(1)}, u32[]{:S(2)}) copy-start(f32[32]{0:T(128)S(1)} %get-tuple-element.200) | copy-start | bytes 388
  25.7 5.2 %copy-start.26 = (f32[32]{0:T(128)}, f32[32]{0:T(128)S(1)}, u32[]{:S(2)}) copy-start(f32[32]{0:T(128)S(1)} %get-tuple-element.197) | copy-start | bytes 388
  25.9 2.9 copy-start.6
  25.9 3.5 %copy-start.8 = (f32[4,768,32]{1,2,0:T(8,128)}, f32[4,768,32]{1,2,0:T(8,128)S(1)}, u32[]{:S(2)}) copy-start(f32[4,768,32]{1,2,0:T(8,128)S(1)} %get-tuple-element.178) | copy-start | bytes 1179652
  25.9 7.5 %copy-start.21 = (f32[32]{0:T(128)S(1)}, f32[32]{0:T(128)}, u32[]{:S(2)}) copy-start(f32[32]{0:T(128)} %param.13) | copy-start | bytes 388
  29.4 0.7 copy-start.14
  30.9 166.4 %all-gather.8.cloned.1.call-start = ((), (), s32[]{:S(2)}) async-start(), calls=%async_computation.1 | async-start | bytes 1114112 | tf_op jit(solution)/shard_map/all_gather | solution.py:15
  34.2 22.8 %copy-start.20 = (pred[768,768]{1,0:T(8,128)(4,1)}, pred[768,768]{1,0:T(8,128)(4,1)S(1)}, u32[]{:S(2)}) copy-start(pred[768,768]{1,0:T(8,128)(4,1)S(1)} %iota_compare_fusion) | copy-start | bytes 1769476
  34.2 22.8 %copy-start.30 = (f32[8]{0:T(128)S(1)}, f32[8]{0:T(128)}, u32[]{:S(2)}) copy-start(f32[8]{0:T(128)} %get-tuple-element.212) | copy-start | bytes 100
  129.1 9.0 %copy-start.11 = (f32[768,768]{1,0:T(8,128)S(1)}, f32[768,768]{1,0:T(8,128)}, u32[]{:S(2)}) copy-start(f32[768,768]{1,0:T(8,128)} %get-tuple-element.139) | copy-start | bytes 7077892
  129.1 9.0 %copy-start.12 = (f32[768,768]{1,0:T(8,128)S(1)}, f32[768,768]{1,0:T(8,128)}, u32[]{:S(2)}) copy-start(f32[768,768]{1,0:T(8,128)} %get-tuple-element.140) | copy-start | bytes 7077892
  129.1 9.0 %copy-start.13 = (f32[768,768]{1,0:T(8,128)S(1)}, f32[768,768]{1,0:T(8,128)}, u32[]{:S(2)}) copy-start(f32[768,768]{1,0:T(8,128)} %get-tuple-element.135) | copy-start | bytes 7077892
  145.2 7.8 %copy-start.10 = (bf16[3072,512]{1,0:T(8,128)(2,1)S(1)}, bf16[3072,512]{1,0:T(8,128)(2,1)}, u32[]{:S(2)}) copy-start(bf16[3072,512]{1,0:T(8,128)(2,1)} %param.11) | copy-start | bytes 9437188
  145.2 7.8 %copy-start.16 = (bf16[1,768,768]{2,1,0:T(8,128)(2,1)S(1)}, bf16[1,768,768]{2,1,0:T(8,128)(2,1)}, u32[]{:S(2)}) copy-start(bf16[1,768,768]{2,1,0:T(8,128)(2,1)} %get-tuple-element.214) | copy-start | bytes 3538948
  145.2 7.8 %copy-start.17 = (bf16[1,768,768]{2,1,0:T(8,128)(2,1)S(1)}, bf16[1,768,768]{2,1,0:T(8,128)(2,1)}, u32[]{:S(2)}) copy-start(bf16[1,768,768]{2,1,0:T(8,128)(2,1)} %get-tuple-element.215) | copy-start | bytes 3538948
  145.2 7.8 %copy-start.18 = (bf16[1,768,768]{2,1,0:T(8,128)(2,1)S(1)}, bf16[1,768,768]{2,1,0:T(8,128)(2,1)}, u32[]{:S(2)}) copy-start(bf16[1,768,768]{2,1,0:T(8,128)(2,1)} %get-tuple-element.216) | copy-start | bytes 3538948
  145.3 7.8 %copy-start.19 = (bf16[1,768,768]{2,1,0:T(8,128)(2,1)S(1)}, bf16[1,768,768]{2,1,0:T(8,128)(2,1)}, u32[]{:S(2)}) copy-start(bf16[1,768,768]{2,1,0:T(8,128)(2,1)} %get-tuple-element.217) | copy-start | bytes 3538948
  153.1 4.9 %copy-start.28 = (f32[1,1,32]{2,1,0:T(1,128)S(1)}, f32[1,1,32]{2,1,0:T(1,128)}, u32[]{:S(2)}) copy-start(f32[1,1,32]{2,1,0:T(1,128)} %get-tuple-element.199) | copy-start | bytes 388
  153.1 28.0 %copy-start.29 = (s32[512]{0:T(512)S(1)}, s32[512]{0:T(512)}, u32[]{:S(2)}) copy-start(s32[512]{0:T(512)} %param.15) | copy-start | bytes 6148
  153.1 32.3 %copy-start.23 = (f32[32]{0:T(128)S(1)}, f32[32]{0:T(128)}, u32[]{:S(2)}) copy-start(f32[32]{0:T(128)} %copy-done.22) | copy-start | bytes 388
  153.1 32.3 %copy-start.27 = (f32[32]{0:T(128)S(1)}, f32[32]{0:T(128)}, u32[]{:S(2)}) copy-start(f32[32]{0:T(128)} %copy-done.26) | copy-start | bytes 388
  181.1 9.3 %copy-start.5 = (f32[4,768,512]{2,1,0:T(8,128)S(1)}, f32[4,768,512]{2,1,0:T(8,128)}, u32[]{:S(2)}) copy-start(f32[4,768,512]{2,1,0:T(8,128)} %fusion.34) | copy-start | bytes 18874372
  181.1 9.3 %copy-start.9 = (f32[4,768,32]{1,2,0:T(8,128)S(1)}, f32[4,768,32]{1,2,0:T(8,128)}, u32[]{:S(2)}) copy-start(f32[4,768,32]{1,2,0:T(8,128)} %copy-done.8) | copy-start | bytes 1179652
  181.1 12.8 %copy-start.25 = (f32[32]{0:T(128)S(1)}, f32[32]{0:T(128)}, u32[]{:S(2)}) copy-start(f32[32]{0:T(128)} %copy-done.24) | copy-start | bytes 388
  211.3 8.1 %copy-start.7 = (f32[4,768,32]{1,2,0:T(8,128)S(1)}, f32[4,768,32]{1,2,0:T(8,128)}, u32[]{:S(2)}) copy-start(f32[4,768,32]{1,2,0:T(8,128)} %copy-done.6) | copy-start | bytes 1179652
  211.4 15.6 %copy-start.1 = (f32[1,768,512]{2,1,0:T(8,128)S(1)}, f32[1,768,512]{2,1,0:T(8,128)}, u32[]{:S(2)}) copy-start(f32[1,768,512]{2,1,0:T(8,128)} %fusion.23) | copy-start | bytes 4718596
  211.4 15.6 %copy-start.2 = (f32[1,768,512]{2,1,0:T(8,128)S(1)}, f32[1,768,512]{2,1,0:T(8,128)}, u32[]{:S(2)}) copy-start(f32[1,768,512]{2,1,0:T(8,128)} %fusion.17) | copy-start | bytes 4718596
  211.5 15.6 %copy-start.3 = (f32[1,768,512]{2,1,0:T(8,128)S(1)}, f32[1,768,512]{2,1,0:T(8,128)}, u32[]{:S(2)}) copy-start(f32[1,768,512]{2,1,0:T(8,128)} %fusion.20) | copy-start | bytes 4718596
  211.5 15.5 %copy-start.4 = (f32[1,768,512]{2,1,0:T(8,128)S(1)}, f32[1,768,512]{2,1,0:T(8,128)}, u32[]{:S(2)}) copy-start(f32[1,768,512]{2,1,0:T(8,128)} %fusion.14) | copy-start | bytes 4718596
Sparse Core Ops, SparseCore 0:
  31.1 40.6 all-gather.5
  73.9 36.8 all-gather.7
